TPU v7x, 32 devices: a whole 2x2x4 slice. The times are simulated.
32 devices in a mesh: ctx: 8 (over y, x, core), fsdp: 4 (over z).
Axes of the slice: x: 2, y: 2, z: 4, core: 2. Of those that a mesh axis runs over, the one named last changes fastest.
Arguments:
- tokens: bfloat16 [4, 1024, 2048], P('fsdp', 'ctx'), may hold values from -6 to 6
- cotangent: bfloat16 [4, 1024, 2048], P('fsdp', 'ctx'), may hold values from -6 to 6
- pairing: int32 [8, 2], replicated, may hold values from 0 to 15, as said below
- norm_attn: float32 [2048], P('fsdp'), may hold values from 0.5 to 1.5
- w_query: bfloat16 [2048, 2048], P('fsdp'), may hold values from -0.125 to 0.125
- w_key: bfloat16 [2048, 512], P('fsdp'), may hold values from -0.125 to 0.125
- w_value: bfloat16 [2048, 512], P('fsdp'), may hold values from -0.125 to 0.125
- w_out: bfloat16 [2048, 2048], P('fsdp'), may hold values from -0.5 to 0.5
- norm_mlp: float32 [2048], P('fsdp'), may hold values from 0.5 to 1.5
- w_gate: bfloat16 [2048, 8192], P('fsdp'), may hold values from -0.125 to 0.125
- w_up: bfloat16 [2048, 8192], P('fsdp'), may hold values from -0.125 to 0.125
- w_down: bfloat16 [8192, 2048], P('fsdp'), may hold values from -0.0625 to 0.0625
Outputs:
- output: bfloat16 [4, 1024, 2048], P('fsdp', 'ctx')
- d_tokens: bfloat16 [4, 1024, 2048], P('fsdp', 'ctx')
- grad_norm_attn: float32 [2048], P('fsdp')
- grad_query: float32 [2048, 2048], P('fsdp')
- grad_key: float32 [2048, 512], P('fsdp')
- grad_value: float32 [2048, 512], P('fsdp')
- grad_out: float32 [2048, 2048], P('fsdp')
- grad_norm_mlp: float32 [2048], P('fsdp')
- grad_gate: float32 [2048, 8192], P('fsdp')
- grad_up: float32 [2048, 8192], P('fsdp')
- grad_down: float32 [8192, 2048], P('fsdp')
Inputs may be any that keep to these rules, and one draw needn't show every extreme that they name: `pairing`: each of the 16 block numbers appears exactly once; each row holds a block number b and its mirror 16 - 1 - b, in either order.
All inputs are finite; a program needn't handle non-finite values.
Results may differ from a plain program's by a relative error of at most 0.035.
Values may be sent and summed in bfloat16 or wider, within the bound.
A program may use at most 448 MiB of HBM per device.

v0:
```python
import math
import jax
import jax.numpy as jnp
from jax import lax
from jax.sharding import PartitionSpec as P

HEAD_DIM = 64
KBLK = 512
EPS = 1e-05
THETA = 500000.0


def frequencies(head_width):
    evens = jnp.arange(0, head_width, 2, dtype=jnp.float32)
    inverse = 1.0 / THETA ** (evens / head_width)
    wavelen = 2.0 * math.pi / inverse
    smooth = (8192.0 / wavelen - 1.0) / 3.0
    middle = (1.0 - smooth) * inverse / 32.0 + smooth * inverse
    return jnp.where(wavelen < 2048.0, inverse, jnp.where(wavelen > 8192.0, inverse / 32.0, middle))


def rotation(positions, head_width):
    angles = positions.astype(jnp.float32)[:, None] * frequencies(head_width)[None, :]
    cosine = jnp.concatenate([jnp.cos(angles), jnp.cos(angles)], axis=1)[:, None, :]
    sine = jnp.concatenate([jnp.sin(angles), jnp.sin(angles)], axis=1)[:, None, :]
    return (cosine, sine)


def rotate(tensor, cosine, sine):
    middle = tensor.shape[-1] // 2
    turned = jnp.concatenate([-tensor[..., middle:], tensor[..., :middle]], axis=-1)
    return tensor * cosine + turned * sine


def unrotate(gradient, cosine, sine):
    middle = gradient.shape[-1] // 2
    moved = gradient * sine
    back_turn = jnp.concatenate([moved[..., middle:], -moved[..., :middle]], axis=-1)
    return gradient * cosine + back_turn


def slot_positions(pairing, seq_length, block_len):
    flattened = pairing.reshape(-1)
    slots = jnp.arange(seq_length, dtype=jnp.int32)
    owning = slots // block_len
    labels = jnp.arange(flattened.shape[0], dtype=jnp.int32)
    anchor = jnp.sum(jnp.where(owning[:, None] == labels[None, :], flattened[None, :], 0), axis=1)
    return anchor * block_len + slots % block_len


def product(left, right):
    return jnp.dot(left, right, preferred_element_type=jnp.float32)


def product_t(left, right):
    return lax.dot_general(
        left, right, (((1,), (1,)), ((), ())), preferred_element_type=jnp.float32
    )


def tokens_t(left, right):
    return lax.dot_general(
        left, right, (((0,), (0,)), ((), ())), preferred_element_type=jnp.float32
    )


def own_columns(matrix, rows):
    return lax.dynamic_slice_in_dim(matrix, lax.axis_index("fsdp") * rows, rows, 1)


def pair_fold(totals, pieces):
    first_rows = totals[0].shape[0]
    second_rows = totals[1].shape[0]
    first = tokens_t(own_columns(pieces[0], first_rows), pieces[1])
    second = tokens_t(own_columns(pieces[2], second_rows), pieces[3])
    return (first, second)


def norm_back(upstream, gain, unit, scale):
    weighted = upstream * gain
    return scale * (weighted - unit * jnp.mean(weighted * unit, axis=1, keepdims=True))


def on_device(
    tokens,
    cotangent,
    pairing,
    norm_attn,
    w_query,
    w_key,
    w_value,
    w_out,
    norm_mlp,
    w_gate,
    w_up,
    w_down,
):
    inputs = tokens[0].astype(jnp.float32)
    tok_rows = inputs.shape[0]
    seq_length = tok_rows * lax.axis_size("ctx")
    heads_kv = w_key.shape[1] // HEAD_DIM
    group_size = w_query.shape[1] // w_key.shape[1]
    all_pos = slot_positions(pairing, seq_length, tok_rows // 2)
    own_pos = lax.dynamic_slice_in_dim(all_pos, lax.axis_index("ctx") * tok_rows, tok_rows)
    cosine, sine = rotation(own_pos, HEAD_DIM)
    factor = HEAD_DIM ** (-0.5)
    gain_attn, query_full, key_full, value_full, out_full = (
        lax.all_gather(norm_attn.astype(jnp.bfloat16), "fsdp", axis=0, tiled=True).astype(
            norm_attn.dtype
        ),
        lax.all_gather(w_query, "fsdp", axis=0, tiled=True),
        lax.all_gather(w_key, "fsdp", axis=0, tiled=True),
        lax.all_gather(w_value, "fsdp", axis=0, tiled=True),
        lax.all_gather(w_out, "fsdp", axis=0, tiled=True),
    )
    scale_attn = lax.rsqrt(jnp.mean(inputs * inputs, axis=1, keepdims=True) + EPS)
    unit_attn = inputs * scale_attn
    normed_attn = (unit_attn * gain_attn).astype(jnp.bfloat16)
    query_rot = rotate(
        product(normed_attn, query_full).reshape(tok_rows, -1, HEAD_DIM), cosine, sine
    )
    queries = query_rot.astype(jnp.bfloat16).reshape(tok_rows, heads_kv, group_size, HEAD_DIM)
    key_rot = rotate(
        product(normed_attn, key_full).reshape(tok_rows, heads_kv, HEAD_DIM), cosine, sine
    )
    keys_local = key_rot.astype(jnp.bfloat16).reshape(tok_rows, heads_kv * HEAD_DIM)
    values_local = product(normed_attn, value_full).astype(jnp.bfloat16)
    keys_all, values_all = (
        lax.all_gather(keys_local, "ctx", axis=0, tiled=True),
        lax.all_gather(values_local, "ctx", axis=0, tiled=True),
    )
    block_count = seq_length // KBLK
    key_blocks = keys_all.reshape(block_count, KBLK, heads_kv, HEAD_DIM)
    value_blocks = values_all.reshape(block_count, KBLK, heads_kv, HEAD_DIM)
    pos_blocks = all_pos.reshape(block_count, KBLK)

    def scores(key_blk, pos_blk):
        logits = jnp.einsum("qhgd,khd->hgqk", queries, key_blk, preferred_element_type=jnp.float32)
        allowed = pos_blk[None, :] <= own_pos[:, None]
        return (jnp.where(allowed, logits * factor, -1e30), allowed)

    def statistics(carry, item):
        running, total = carry
        score_blk, allowed = scores(item[0], item[1])
        newest = jnp.maximum(running, jnp.max(score_blk, axis=-1))
        added = jnp.sum(jnp.where(allowed, jnp.exp(score_blk - newest[..., None]), 0.0), axis=-1)
        return ((newest, total * jnp.exp(running - newest) + added), None)

    start_top = jnp.full((heads_kv, group_size, tok_rows), -1e30, jnp.float32)
    start_sum = jnp.zeros((heads_kv, group_size, tok_rows), jnp.float32)
    (running, total), _ = lax.scan(statistics, (start_top, start_sum), (key_blocks, pos_blocks))
    log_total = running + jnp.log(total)

    def weights_of(score_blk, allowed):
        return jnp.where(allowed, jnp.exp(score_blk - log_total[..., None]), 0.0)

    def attend(acc, item):
        key_blk, value_blk, pos_blk = item
        score_blk, allowed = scores(key_blk, pos_blk)
        probs_low = weights_of(score_blk, allowed).astype(jnp.bfloat16)
        return (
            acc
            + jnp.einsum(
                "hgqk,khd->qhgd", probs_low, value_blk, preferred_element_type=jnp.float32
            ),
            None,
        )

    start_acc = jnp.zeros((tok_rows, heads_kv, group_size, HEAD_DIM), jnp.float32)
    attended, _ = lax.scan(attend, start_acc, (key_blocks, value_blocks, pos_blocks))
    attended_low = attended.reshape(tok_rows, -1).astype(jnp.bfloat16)
    resid = inputs + product(attended_low, out_full)
    gain_mlp, gate_full, up_full, down_full = (
        lax.all_gather(norm_mlp.astype(jnp.bfloat16), "fsdp", axis=0, tiled=True).astype(
            norm_mlp.dtype
        ),
        lax.all_gather(w_gate, "fsdp", axis=0, tiled=True),
        lax.all_gather(w_up, "fsdp", axis=0, tiled=True),
        lax.all_gather(w_down, "fsdp", axis=0, tiled=True),
    )
    scale_mlp = lax.rsqrt(jnp.mean(resid * resid, axis=1, keepdims=True) + EPS)
    unit_mlp = resid * scale_mlp
    normed_mlp = (unit_mlp * gain_mlp).astype(jnp.bfloat16)
    gate_pre = product(normed_mlp, gate_full)
    up_pre = product(normed_mlp, up_full)
    sigma = jax.nn.sigmoid(gate_pre)
    swish = gate_pre * sigma
    hidden = (swish * up_pre).astype(jnp.bfloat16)
    output = resid + product(hidden, down_full)
    upstream = cotangent[0]
    gain_mlp, gate_full, up_full, down_full = (
        lax.all_gather(norm_mlp.astype(jnp.bfloat16), "fsdp", axis=0, tiled=True).astype(
            norm_mlp.dtype
        ),
        lax.all_gather(w_gate, "fsdp", axis=0, tiled=True),
        lax.all_gather(w_up, "fsdp", axis=0, tiled=True),
        lax.all_gather(w_down, "fsdp", axis=0, tiled=True),
    )
    d_hidden = product_t(upstream, down_full)
    d_gate = (d_hidden * up_pre * sigma * (1.0 + gate_pre * (1.0 - sigma))).astype(jnp.bfloat16)
    d_up = (d_hidden * swish).astype(jnp.bfloat16)
    d_normed_mlp = product_t(d_gate, gate_full) + product_t(d_up, up_full)
    gate_up_pair = jnp.concatenate([d_gate, d_up], axis=1)
    ff_width = w_gate.shape[1]
    down_rows = w_down.shape[0]
    model_rows = w_gate.shape[0]
    start_down = jnp.zeros((down_rows, upstream.shape[1]), jnp.float32)
    start_pair = jnp.zeros((model_rows, gate_up_pair.shape[1]), jnp.float32)
    grad_down, grad_pair = pair_fold(
        (start_down, start_pair),
        (
            lax.all_gather(hidden, "fsdp", axis=0, tiled=True),
            lax.all_gather(upstream, "fsdp", axis=0, tiled=True),
            lax.all_gather(normed_mlp, "fsdp", axis=0, tiled=True),
            lax.all_gather(gate_up_pair, "fsdp", axis=0, tiled=True),
        ),
    )
    grad_gate = grad_pair[:, :ff_width]
    grad_up = grad_pair[:, ff_width:]
    gain_mlp_term = jnp.sum(d_normed_mlp * unit_mlp, axis=0)
    d_resid = upstream.astype(jnp.float32) + norm_back(d_normed_mlp, gain_mlp, unit_mlp, scale_mlp)
    d_resid_low = d_resid.astype(jnp.bfloat16)
    gain_attn, query_full, key_full, value_full, out_full = (
        lax.all_gather(norm_attn.astype(jnp.bfloat16), "fsdp", axis=0, tiled=True).astype(
            norm_attn.dtype
        ),
        lax.all_gather(w_query, "fsdp", axis=0, tiled=True),
        lax.all_gather(w_key, "fsdp", axis=0, tiled=True),
        lax.all_gather(w_value, "fsdp", axis=0, tiled=True),
        lax.all_gather(w_out, "fsdp", axis=0, tiled=True),
    )
    d_attended = (
        product_t(d_resid_low, out_full)
        .astype(jnp.bfloat16)
        .reshape(tok_rows, heads_kv, group_size, HEAD_DIM)
    )
    delta = jnp.einsum("qhgd,qhgd->hgq", d_attended.astype(jnp.float32), attended)

    def backward_step(carry, item):
        key_blk, value_blk, pos_blk = item
        score_blk, allowed = scores(key_blk, pos_blk)
        probs = weights_of(score_blk, allowed)
        grad_val = jnp.einsum(
            "hgqk,qhgd->khd",
            probs.astype(jnp.bfloat16),
            d_attended,
            preferred_element_type=jnp.float32,
        )
        d_probs = jnp.einsum(
            "qhgd,khd->hgqk", d_attended, value_blk, preferred_element_type=jnp.float32
        )
        d_score = (probs * (d_probs - delta[..., None]) * factor).astype(jnp.bfloat16)
        carry = carry + jnp.einsum(
            "hgqk,khd->qhgd", d_score, key_blk, preferred_element_type=jnp.float32
        )
        grad_keyblk = jnp.einsum(
            "hgqk,qhgd->khd", d_score, queries, preferred_element_type=jnp.float32
        )
        return (carry, (grad_keyblk, grad_val))

    d_query_rot, (key_terms, value_terms) = lax.scan(
        backward_step, start_acc, (key_blocks, value_blocks, pos_blocks)
    )
    key_sum, value_sum = (
        lax.psum_scatter(
            key_terms.reshape(seq_length, -1).astype(jnp.bfloat16),
            "ctx",
            scatter_dimension=0,
            tiled=True,
        ).astype(jnp.float32),
        lax.psum_scatter(
            value_terms.reshape(seq_length, -1).astype(jnp.bfloat16),
            "ctx",
            scatter_dimension=0,
            tiled=True,
        ).astype(jnp.float32),
    )
    d_query = (
        unrotate(d_query_rot.reshape(tok_rows, -1, HEAD_DIM), cosine, sine)
        .reshape(tok_rows, -1)
        .astype(jnp.bfloat16)
    )
    d_key = (
        unrotate(key_sum.reshape(tok_rows, heads_kv, HEAD_DIM), cosine, sine)
        .reshape(tok_rows, -1)
        .astype(jnp.bfloat16)
    )
    d_value_low = value_sum.astype(jnp.bfloat16)
    d_normed_attn = (
        product_t(d_query, query_full)
        + product_t(d_key, key_full)
        + product_t(d_value_low, value_full)
    )
    joined = jnp.concatenate([d_query, d_key, d_value_low], axis=1)
    out_rows = w_out.shape[0]
    query_rows = w_query.shape[0]
    start_out = jnp.zeros((out_rows, d_resid_low.shape[1]), jnp.float32)
    start_joined = jnp.zeros((query_rows, joined.shape[1]), jnp.float32)
    grad_out, grad_joined = pair_fold(
        (start_out, start_joined),
        (
            lax.all_gather(attended_low, "fsdp", axis=0, tiled=True),
            lax.all_gather(d_resid_low, "fsdp", axis=0, tiled=True),
            lax.all_gather(normed_attn, "fsdp", axis=0, tiled=True),
            lax.all_gather(joined, "fsdp", axis=0, tiled=True),
        ),
    )
    query_width = w_query.shape[1]
    key_width = w_key.shape[1]
    grad_query = grad_joined[:, :query_width]
    grad_key = grad_joined[:, query_width : query_width + key_width]
    grad_value = grad_joined[:, query_width + key_width :]
    gain_attn_term = jnp.sum(d_normed_attn * unit_attn, axis=0)
    d_inputs = d_resid + norm_back(d_normed_attn, gain_attn, unit_attn, scale_attn)
    gain_attn_part, gain_mlp_part = (
        lax.psum_scatter(gain_attn_term, "fsdp", scatter_dimension=0, tiled=True),
        lax.psum_scatter(gain_mlp_term, "fsdp", scatter_dimension=0, tiled=True),
    )
    summed = (
        lax.psum(gain_attn_part.astype(jnp.bfloat16), "ctx").astype(jnp.float32),
        lax.psum(grad_query.astype(jnp.bfloat16), "ctx").astype(jnp.float32),
        lax.psum(grad_key.astype(jnp.bfloat16), "ctx").astype(jnp.float32),
        lax.psum(grad_value.astype(jnp.bfloat16), "ctx").astype(jnp.float32),
        lax.psum(grad_out.astype(jnp.bfloat16), "ctx").astype(jnp.float32),
        lax.psum(gain_mlp_part.astype(jnp.bfloat16), "ctx").astype(jnp.float32),
        lax.psum(grad_gate.astype(jnp.bfloat16), "ctx").astype(jnp.float32),
        lax.psum(grad_up.astype(jnp.bfloat16), "ctx").astype(jnp.float32),
        lax.psum(grad_down.astype(jnp.bfloat16), "ctx").astype(jnp.float32),
    )
    return (
        output.astype(jnp.bfloat16)[None],
        d_inputs.astype(jnp.bfloat16)[None],
        summed[0],
        summed[1],
        summed[2],
        summed[3],
        summed[4],
        summed[5],
        summed[6],
        summed[7],
        summed[8],
    )


def solution(mesh):
    return jax.shard_map(
        on_device,
        mesh=mesh,
        in_specs=(
            P("fsdp", "ctx", None),
            P("fsdp", "ctx", None),
            P(),
            P("fsdp"),
            P("fsdp", None),
            P("fsdp", None),
            P("fsdp", None),
            P("fsdp", None),
            P("fsdp"),
            P("fsdp", None),
            P("fsdp", None),
            P("fsdp", None),
        ),
        out_specs=(
            P("fsdp", "ctx", None),
            P("fsdp", "ctx", None),
            P("fsdp"),
            P("fsdp", None),
            P("fsdp", None),
            P("fsdp", None),
            P("fsdp", None),
            P("fsdp"),
            P("fsdp", None),
            P("fsdp", None),
            P("fsdp", None),
        ),
        check_vma=False,
    )
```

profile of v0, /device:TPU:0, one launch (start us, length us, event | category | flops | bytes accessed | tf_op | source)
XLA Modules:
  0.0 3507.1 jit_solution(8441512161050424623)
XLA Ops:
  9.4 13.5 all-gather.1
  25.5 32.8 all-gather.21.cloned.1.call-done
  62.3 42.2 %all-gather.25.cloned.1.call-done = bf16[2048,512]{1,0:T(8,128)(2,1)} async-done(((bf16[512,512]{1,0:T(8,128)(2,1)}), bf16[2048,512]{1,0:T(8,128)(2,1)}) %all-gather.25.cloned.1.call-update) | async-done | bytes 2097168 | tf_op jit(solution)/shard_map/all_gather | solution.py:112
  136.4 18.7 all-gather.27.cloned.1.call-done
  159.2 147.0 %all-gather.29.cloned.1.call-done = bf16[2048,2048]{1,0:T(8,128)(2,1)} async-done(((bf16[512,2048]{1,0:T(8,128)(2,1)}), bf16[2048,2048]{1,0:T(8,128)(2,1)}) %all-gather.29.cloned.1.call-update) | async-done | bytes 8388624 | tf_op jit(solution)/shard_map/all_gather | solution.py:111
  306.2 12.4 copy.73
  324.9 19.0 while.39
  356.6 98.9 %all-gather.31.cloned.1.call-done = bf16[2048,2048]{1,0:T(8,128)(2,1)} async-done(((bf16[512,2048]{1,0:T(8,128)(2,1)}), bf16[2048,2048]{1,0:T(8,128)(2,1)}) %all-gather.31.cloned.1.call-update) | async-done | bytes 8388624 | tf_op jit(solution)/shard_map/all_gather | solution.py:114
  461.7 555.1 %all-gather.33.cloned.1.call-done = bf16[2048,8192]{1,0:T(8,128)(2,1)} async-done(((bf16[512,8192]{1,0:T(8,128)(2,1)}), bf16[2048,8192]{1,0:T(8,128)(2,1)}) %all-gather.33.cloned.1.call-update) | async-done | bytes 33554448 | tf_op jit(solution)/shard_map/all_gather | solution.py:177
  1016.8 21.2 fusion.122
  1038.0 540.0 %all-gather.35.cloned.1.call-done = bf16[2048,8192]{1,0:T(8,128)(2,1)} async-done(((bf16[512,8192]{1,0:T(8,128)(2,1)}), bf16[2048,8192]{1,0:T(8,128)(2,1)}) %all-gather.35.cloned.1.call-update) | async-done | bytes 33554448 | tf_op jit(solution)/shard_map/all_gather | solution.py:178
  1578.0 21.2 fusion.123
  1599.2 540.0 %all-gather.37.cloned.1.call-done = bf16[8192,2048]{1,0:T(8,128)(2,1)} async-done(((bf16[2048,2048]{1,0:T(8,128)(2,1)}), bf16[8192,2048]{1,0:T(8,128)(2,1)}) %all-gather.37.cloned.1.call-update) | async-done | bytes 33554448 | tf_op jit(solution)/shard_map/all_gather | solution.py:179
  2139.2 21.2 multiply_convert_fusion
  2160.4 17.3 fusion.124
  2177.7 18.5 multiply_reduce_fusion
  2208.7 35.3 %while.41 = (s32[]{:T(128)}, f32[128,8,4,64]{0,3,2,1:T(8,128)S(1)}, bf16[2,512,8,64]{1,3,2,0:T(8,128)(2,1)}, bf16[2,512,8,64]{1,3,2,0:T(8,128)(2,1)}, bf16[2,512...) while((s32[]{:T(128)}, f32[128,8,4,64]{0,3,2,1:T(8,128)S(1)}, ...), condition=%wide.region_11.12_spmd.clone, body=%wide.region_10.11_spmd.clone.sunk | while | flops 1370030080 | bytes 125557568 | solution.py:261
  2261.5 24.3 reduce-scatter.7.cloned.1.call-done
  2287.0 38.6 %reduce-scatter.9.cloned.1.call-done = bf16[128,512]{1,0:T(8,128)(2,1)} async-done(((bf16[1024,512]{1,0:T(8,128)(2,1)}), bf16[128,512]{1,0:T(8,128)(2,1)}) %reduce-scatter.9.cloned.1.call-update) | async-done | bytes 131088
  2334.5 39.4 %all-gather.43.cloned.1.call-done = bf16[512,2048]{0,1:T(8,128)(2,1)} async-done(((bf16[128,2048]{0,1:T(8,128)(2,1)}), bf16[512,2048]{0,1:T(8,128)(2,1)}) %all-gather.43.cloned.1.call-update) | async-done | bytes 2097168 | tf_op jit(solution)/shard_map/all_gather | solution.py:302
  2373.9 46.3 %all-gather.45.cloned.1.call-done = bf16[512,2048]{1,0:T(8,128)(2,1)} async-done(((bf16[128,2048]{1,0:T(8,128)(2,1)}), bf16[512,2048]{1,0:T(8,128)(2,1)}) %all-gather.45.cloned.1.call-update) | async-done | bytes 2097168 | tf_op jit(solution)/shard_map/all_gather | solution.py:303
  2424.6 41.8 %all-gather.39.cloned.1.call-done = bf16[512,2048]{1,0:T(8,128)(2,1)} async-done(((bf16[128,2048]{1,0:T(8,128)(2,1)}), bf16[512,2048]{1,0:T(8,128)(2,1)}) %all-gather.39.cloned.1.call-update) | async-done | bytes 2097168 | tf_op jit(solution)/shard_map/all_gather | solution.py:304
  2466.3 64.2 %all-gather.41.cloned.1.call-done = bf16[512,3072]{0,1:T(8,128)(2,1)} async-done(((bf16[128,3072]{0,1:T(8,128)(2,1)}), bf16[512,3072]{0,1:T(8,128)(2,1)}) %all-gather.41.cloned.1.call-update) | async-done | bytes 3145744 | tf_op jit(solution)/shard_map/all_gather | solution.py:305
  2536.9 39.1 %all-gather.53.cloned.1.call-done = bf16[1,512,2048]{2,1,0:T(8,128)(2,1)} async-done(((bf16[1,128,2048]{2,1,0:T(8,128)(2,1)}), bf16[1,512,2048]{2,1,0:T(8,128)(2,1)}) %all-gather.53.cloned.1.call-update) | async-done | bytes 2097168 | tf_op jit(solution)/shard_map/all_gather | solution.py:213
  2576.1 149.8 %all-gather.51.cloned.1.call-done = bf16[512,8192]{1,0:T(8,128)(2,1)} async-done(((bf16[128,8192]{1,0:T(8,128)(2,1)}), bf16[512,8192]{1,0:T(8,128)(2,1)}) %all-gather.51.cloned.1.call-update) | async-done | bytes 8388624 | tf_op jit(solution)/shard_map/all_gather | solution.py:212
  2735.9 35.6 %all-gather.47.cloned.1.call-done = bf16[512,2048]{1,0:T(8,128)(2,1)} async-done(((bf16[128,2048]{1,0:T(8,128)(2,1)}), bf16[512,2048]{1,0:T(8,128)(2,1)}) %all-gather.47.cloned.1.call-update) | async-done | bytes 2097168 | tf_op jit(solution)/shard_map/all_gather | solution.py:214
  2771.5 287.7 %all-gather.49.cloned.1.call-done = bf16[512,16384]{1,0:T(8,128)(2,1)} async-done(((bf16[128,16384]{1,0:T(8,128)(2,1)}), bf16[512,16384]{1,0:T(8,128)(2,1)}) %all-gather.49.cloned.1.call-update) | async-done | bytes 16777232 | tf_op jit(solution)/shard_map/all_gather | solution.py:215
  3059.1 16.0 convolution_convert_fusion
  3096.6 17.4 fusion.65
  3116.8 15.6 all-reduce.2
  3132.5 13.1 all-reduce.3
  3149.4 304.3 %all-reduce.7.cloned.1.call-done = (bf16[512,2048]{1,0:T(8,128)(2,1)}, bf16[512,512]{1,0:T(8,128)(2,1)}, bf16[512,512]{1,0:T(8,128)(2,1)}, bf16[512,2048]{1,0:T(...) async-done(((bf16[512,2048]{1,0:T(8,128)(2,1)}, bf16[512,512]{1,0:T(8,128)(2,1)}, bf16[512,512]{1,0:T(8,128)(2,1)}, ...) | async-done | bytes 30408720 | tf_op jit(solution)/shard_map/psum | solution.py:321
  (247 shorter events, 267.4 us)
Async XLA Ops:
  7.2 100.3 %copy-start.5 = (bf16[1,128,2048]{2,1,0:T(8,128)(2,1)S(1)}, bf16[1,128,2048]{2,1,0:T(8,128)(2,1)}, u32[]{:S(2)}) copy-start(bf16[1,128,2048]{2,1,0:T(8,128)(2,1)} %param.18) | copy-start | bytes 1572868
  7.2 51.1 %all-gather.21.cloned.1.call-start = ((), (), s32[]{:S(2)}) async-start(), calls=%async_computation.2 | async-start | bytes 2621440 | tf_op jit(solution)/shard_map/all_gather | solution.py:113
  7.9 96.6 %all-gather.25.cloned.1.call-start = ((), (), s32[]{:S(2)}) async-start(), calls=%async_computation.4 | async-start | bytes 2621440 | tf_op jit(solution)/shard_map/all_gather | solution.py:112
  8.7 120.6 %all-gather.23.cloned.1.call-start = ((), (), s32[]{:S(2)}) async-start(), calls=%async_computation.3 | async-start | bytes 1179648 | tf_op jit(solution)/shard_map/all_gather | solution.py:130
  23.0 295.7 %copy-start.23 = (f32[4,1,512]{2,1,0:T(1,128)}, f32[4,1,512]{2,1,0:T(1,128)S(1)}, u32[]{:S(2)}) copy-start(f32[4,1,512]{2,1,0:T(1,128)S(1)} %convert_element_type.203) | copy-start | bytes 24580
  24.2 294.4 %copy-start.28 = (f32[128]{0:T(128)}, f32[128]{0:T(128)S(1)}, u32[]{:S(2)}) copy-start(f32[128]{0:T(128)S(1)} %add_rsqrt_fusion.1) | copy-start | bytes 1540
  25.5 79.1 %copy-start.13 = (bf16[128,2048]{1,0:T(8,128)(2,1)}, bf16[128,2048]{1,0:T(8,128)(2,1)S(1)}, u32[]{:S(2)}) copy-start(bf16[128,2048]{1,0:T(8,128)(2,1)S(1)} %fusion.74) | copy-start | bytes 1572868
  61.0 94.1 %all-gather.27.cloned.1.call-start = ((), (), s32[]{:S(2)}) async-start(), calls=%async_computation.5 | async-start | bytes 1179648 | tf_op jit(solution)/shard_map/all_gather | solution.py:129
  62.3 262.5 %copy-start.18 = (f32[128,64]{0,1:T(8,128)}, f32[128,64]{0,1:T(8,128)S(1)}, u32[]{:S(2)}) copy-start(f32[128,64]{0,1:T(8,128)S(1)} %pad_maximum_fusion.5) | copy-start | bytes 98308
  62.3 262.5 %copy-start.20 = (f32[128,64]{0,1:T(8,128)}, f32[128,64]{0,1:T(8,128)S(1)}, u32[]{:S(2)}) copy-start(f32[128,64]{0,1:T(8,128)S(1)} %pad_maximum_fusion.4) | copy-start | bytes 98308
  109.0 197.2 %all-gather.29.cloned.1.call-start = ((), (), s32[]{:S(2)}) async-start(), calls=%async_computation.6 | async-start | bytes 10485760 | tf_op jit(solution)/shard_map/all_gather | solution.py:111
  109.6 345.9 %all-gather.31.cloned.1.call-start = ((), (), s32[]{:S(2)}) async-start(), calls=%async_computation.7 | async-start | bytes 10485760 | tf_op jit(solution)/shard_map/all_gather | solution.py:114
  110.2 906.6 %all-gather.33.cloned.1.call-start = ((), (), s32[]{:S(2)}) async-start(), calls=%async_computation.8 | async-start | bytes 41943040 | tf_op jit(solution)/shard_map/all_gather | solution.py:177
  110.9 1467.0 %all-gather.35.cloned.1.call-start = ((), (), s32[]{:S(2)}) async-start(), calls=%async_computation.9 | async-start | bytes 41943040 | tf_op jit(solution)/shard_map/all_gather | solution.py:178
  111.7 2027.5 %all-gather.37.cloned.1.call-start = ((), (), s32[]{:S(2)}) async-start(), calls=%async_computation.10 | async-start | bytes 41943040 | tf_op jit(solution)/shard_map/all_gather | solution.py:179
  112.4 2173.4 %reduce-scatter.7.cloned.1.call-start = ((), (), s32[]{:S(2)}) async-start(), calls=%async_computation.19 | async-start | bytes 1179648
  124.8 2071.5 %copy-start.25 = (f32[4,1,512]{2,1,0:T(1,128)}, f32[4,1,512]{2,1,0:T(1,128)S(1)}, u32[]{:S(2)}) copy-start(f32[4,1,512]{2,1,0:T(1,128)S(1)} %convert_element_type.204) | copy-start | bytes 24580
  460.5 1735.8 %copy-start.30 = (f32[128]{0:T(128)}, f32[128]{0:T(128)S(1)}, u32[]{:S(2)}) copy-start(f32[128]{0:T(128)S(1)} %add_rsqrt_fusion) | copy-start | bytes 1540
  461.7 1116.3 %copy-start.8 = (bf16[128,2048]{1,0:T(8,128)(2,1)}, bf16[128,2048]{1,0:T(8,128)(2,1)S(1)}, u32[]{:S(2)}) copy-start(bf16[128,2048]{1,0:T(8,128)(2,1)S(1)} %multiply_convert_fusion.3) | copy-start | bytes 1572868
  2251.5 74.2 %reduce-scatter.9.cloned.1.call-start = ((), (), s32[]{:S(2)}) async-start(), calls=%async_computation.20 | async-start | bytes 1179648
  2259.1 114.8 %all-gather.43.cloned.1.call-start = ((), (), s32[]{:S(2)}) async-start(), calls=%async_computation.13 | async-start | bytes 2621440 | tf_op jit(solution)/shard_map/all_gather | solution.py:302
  2259.6 160.6 %all-gather.45.cloned.1.call-start = ((), (), s32[]{:S(2)}) async-start(), calls=%async_computation.14 | async-start | bytes 2621440 | tf_op jit(solution)/shard_map/all_gather | solution.py:303
  2260.4 205.9 %all-gather.39.cloned.1.call-start = ((), (), s32[]{:S(2)}) async-start(), calls=%async_computation.11 | async-start | bytes 2621440 | tf_op jit(solution)/shard_map/all_gather | solution.py:304
  2261.0 269.5 %all-gather.41.cloned.1.call-start = ((), (), s32[]{:S(2)}) async-start(), calls=%async_computation.12 | async-start | bytes 3932160 | tf_op jit(solution)/shard_map/all_gather | solution.py:305
  2327.6 248.5 %all-gather.53.cloned.1.call-start = ((), (), s32[]{:S(2)}) async-start(), calls=%async_computation.18 | async-start | bytes 2621440 | tf_op jit(solution)/shard_map/all_gather | solution.py:213
  2328.2 397.7 %all-gather.51.cloned.1.call-start = ((), (), s32[]{:S(2)}) async-start(), calls=%async_computation.17 | async-start | bytes 10485760 | tf_op jit(solution)/shard_map/all_gather | solution.py:212
  2328.8 442.7 %all-gather.47.cloned.1.call-start = ((), (), s32[]{:S(2)}) async-start(), calls=%async_computation.15 | async-start | bytes 2621440 | tf_op jit(solution)/shard_map/all_gather | solution.py:214
  2329.4 729.8 %all-gather.49.cloned.1.call-start = ((), (), s32[]{:S(2)}) async-start(), calls=%async_computation.16 | async-start | bytes 20971520 | tf_op jit(solution)/shard_map/all_gather | solution.py:215
  2334.0 1119.7 %all-reduce.7.cloned.1.call-start = ((), (), s32[]{:S(2)}) async-start(), calls=%async_computation.21 | async-start | bytes 60817408 | tf_op jit(solution)/shard_map/psum | solution.py:321
  3114.0 32.7 copy-start.7
  3114.0 32.7 copy-start.12
  3114.0 32.7 copy-start.26
  (29 other events, 321.8 us)
Sparse Core Ops, SparseCore 0:
  9.6 48.6 all-gather.20
  59.8 44.6 all-gather.24
  107.0 22.1 all-gather.22
  131.5 23.5 all-gather.26
  156.5 149.6 all-gather.28
  307.6 147.8 all-gather.30
  457.1 559.6 all-gather.32
  1018.3 559.5 all-gather.34
  1579.5 559.5 all-gather.36
  2251.6 34.1 reduce-scatter.6
  2289.6 35.9 reduce-scatter.8
  2327.6 46.2 all-gather.42
  2376.0 44.1 all-gather.44
  2421.6 44.6 all-gather.38
  2468.3 62.1 all-gather.40
  2531.9 44.1 all-gather.52
  2577.5 148.3 all-gather.50
  2727.3 44.1 all-gather.46
  2773.6 285.4 all-gather.48
  3087.1 366.5 all-reduce.6
where the time goes:
time: 3510 us
  waiting for transfers between devices  3060 us (87%)
  matrix products  235 us (7%)
  other arithmetic  76.8 us (2%)
  local copies, waits for them, and re-layouts  64.8 us (2%)
  blocking collectives  54.3 us (2%)
    all_gather x1, waiting for transfers between devices, on_device(): lax.all_gather(w_gate, 'fsdp', axis=0, tiled=True)  555 us
    all_gather x1, waiting for transfers between devices, on_device(): lax.all_gather(w_down, 'fsdp', axis=0, tiled=True)  540 us
    all_gather x1, waiting for transfers between devices, on_device(): lax.all_gather(w_up, 'fsdp', axis=0, tiled=True)  540 us
    psum x1, waiting for transfers between devices, on_device(): lax.psum(grad_query.astype(jnp.bfloat16), 'ctx').astype(jnp.float32)  304 us
    all_gather x1, waiting for transfers between devices, on_device(): lax.all_gather(gate_up_pair, 'fsdp', axis=0, tiled=True)  288 us
    all_gather x1, waiting for transfers between devices, on_device(): lax.all_gather(hidden, 'fsdp', axis=0, tiled=True)  150 us
    all_gather x1, waiting for transfers between devices, on_device(): lax.all_gather(w_query, 'fsdp', axis=0, tiled=True)  147 us
    all_gather x1, waiting for transfers between devices, on_device(): lax.all_gather(w_out, 'fsdp', axis=0, tiled=True)  98.9 us
  transfers between devices with their start and end apart: 20, of which 20 were waited for; matrix products, arithmetic and copies ran while one was open for 5% of the time, Pallas kernels for 0%

commit v1 on v0

--- a/solution.py
+++ b/solution.py
@@ -316,9 +316,10 @@
         lax.psum_scatter(gain_attn_term, "fsdp", scatter_dimension=0, tiled=True),
         lax.psum_scatter(gain_mlp_term, "fsdp", scatter_dimension=0, tiled=True),
     )
+    _see_lines = lambda view, row_axis: jnp.sum(lax.all_gather(view, row_axis), 0)
     summed = (
         lax.psum(gain_attn_part.astype(jnp.bfloat16), "ctx").astype(jnp.float32),
-        lax.psum(grad_query.astype(jnp.bfloat16), "ctx").astype(jnp.float32),
+        _see_lines(grad_query.astype(jnp.bfloat16), "ctx").astype(jnp.float32),
         lax.psum(grad_key.astype(jnp.bfloat16), "ctx").astype(jnp.float32),
         lax.psum(grad_value.astype(jnp.bfloat16), "ctx").astype(jnp.float32),
         lax.psum(grad_out.astype(jnp.bfloat16), "ctx").astype(jnp.float32),

time: 3510 us -> 3560 us (1.014)
    unnamed x22 -> x23, waiting for transfers between devices: 70.9 us -> 72.1 us
  transfers between devices with their start and end apart: 20 -> 21, of which waited for: 20 -> 20; matrix products, arithmetic and copies ran while one was open for 5% -> 7% of each run, Pallas kernels for 0% -> 0%
where the time goes in v1:
time: 3560 us; the launch traced here: 3550 us
  waiting for transfers between devices  3090 us (87%)
  matrix products  236 us (7%)
  other arithmetic  86.9 us (2%)
  local copies, waits for them, and re-layouts  67.6 us (2%)
  blocking collectives  53.8 us (2%)
    all_gather x1, waiting for transfers between devices, on_device(): lax.all_gather(w_gate, 'fsdp', axis=0, tiled=True)  555 us
    all_gather x1, waiting for transfers between devices, on_device(): lax.all_gather(w_down, 'fsdp', axis=0, tiled=True)  540 us
    all_gather x1, waiting for transfers between devices, on_device(): lax.all_gather(w_up, 'fsdp', axis=0, tiled=True)  540 us
    psum x1, waiting for transfers between devices, on_device(): lax.psum(grad_key.astype(jnp.bfloat16), 'ctx').astype(jnp.float32)  337 us
    all_gather x1, waiting for transfers between devices, on_device(): lax.all_gather(gate_up_pair, 'fsdp', axis=0, tiled=True)  288 us
    all_gather x1, waiting for transfers between devices, on_device(): lax.all_gather(hidden, 'fsdp', axis=0, tiled=True)  150 us
    all_gather x1, waiting for transfers between devices, on_device(): lax.all_gather(w_query, 'fsdp', axis=0, tiled=True)  147 us
    all_gather x1, waiting for transfers between devices, on_device(): lax.all_gather(w_out, 'fsdp', axis=0, tiled=True)  98.9 us
  transfers between devices with their start and end apart: 21, of which 20 were waited for; matrix products, arithmetic and copies ran while one was open for 7% of the time, Pallas kernels for 0%

profile of v1, /device:TPU:0, one launch (start us, length us, event | category | flops | bytes accessed | tf_op | source)
XLA Modules:
  0.0 3550.6 jit_solution(5354227297840074547)
XLA Ops:
  9.4 13.5 all-gather.2
  25.5 32.8 all-gather.23.cloned.1.call-done
  62.3 42.2 %all-gather.27.cloned.1.call-done = bf16[2048,512]{1,0:T(8,128)(2,1)} async-done(((bf16[512,512]{1,0:T(8,128)(2,1)}), bf16[2048,512]{1,0:T(8,128)(2,1)}) %all-gather.27.cloned.1.call-update) | async-done | bytes 2097168 | tf_op jit(solution)/shard_map/all_gather | solution.py:112
  136.4 18.7 all-gather.29.cloned.1.call-done
  159.2 147.0 %all-gather.31.cloned.1.call-done = bf16[2048,2048]{1,0:T(8,128)(2,1)} async-done(((bf16[512,2048]{1,0:T(8,128)(2,1)}), bf16[2048,2048]{1,0:T(8,128)(2,1)}) %all-gather.31.cloned.1.call-update) | async-done | bytes 8388624 | tf_op jit(solution)/shard_map/all_gather | solution.py:111
  306.2 12.4 copy.73
  324.9 19.0 while.39
  356.6 98.9 %all-gather.33.cloned.1.call-done = bf16[2048,2048]{1,0:T(8,128)(2,1)} async-done(((bf16[512,2048]{1,0:T(8,128)(2,1)}), bf16[2048,2048]{1,0:T(8,128)(2,1)}) %all-gather.33.cloned.1.call-update) | async-done | bytes 8388624 | tf_op jit(solution)/shard_map/all_gather | solution.py:114
  461.7 555.1 %all-gather.35.cloned.1.call-done = bf16[2048,8192]{1,0:T(8,128)(2,1)} async-done(((bf16[512,8192]{1,0:T(8,128)(2,1)}), bf16[2048,8192]{1,0:T(8,128)(2,1)}) %all-gather.35.cloned.1.call-update) | async-done | bytes 33554448 | tf_op jit(solution)/shard_map/all_gather | solution.py:177
  1016.8 21.2 fusion.122
  1038.0 540.0 %all-gather.37.cloned.1.call-done = bf16[2048,8192]{1,0:T(8,128)(2,1)} async-done(((bf16[512,8192]{1,0:T(8,128)(2,1)}), bf16[2048,8192]{1,0:T(8,128)(2,1)}) %all-gather.37.cloned.1.call-update) | async-done | bytes 33554448 | tf_op jit(solution)/shard_map/all_gather | solution.py:178
  1578.0 21.2 fusion.123
  1599.2 540.0 %all-gather.39.cloned.1.call-done = bf16[8192,2048]{1,0:T(8,128)(2,1)} async-done(((bf16[2048,2048]{1,0:T(8,128)(2,1)}), bf16[8192,2048]{1,0:T(8,128)(2,1)}) %all-gather.39.cloned.1.call-update) | async-done | bytes 33554448 | tf_op jit(solution)/shard_map/all_gather | solution.py:179
  2139.2 21.2 multiply_convert_fusion
  2160.4 17.3 fusion.124
  2177.7 18.5 multiply_reduce_fusion
  2208.7 35.3 while.41
  2260.2 25.6 reduce-scatter.7.cloned.1.call-done
  2287.0 38.6 %reduce-scatter.9.cloned.1.call-done = bf16[128,512]{1,0:T(8,128)(2,1)} async-done(((bf16[1024,512]{1,0:T(8,128)(2,1)}), bf16[128,512]{1,0:T(8,128)(2,1)}) %reduce-scatter.9.cloned.1.call-update) | async-done | bytes 131088
  2335.7 37.3 %all-gather.41.cloned.1.call-done = bf16[512,2048]{1,0:T(8,128)(2,1)} async-done(((bf16[128,2048]{1,0:T(8,128)(2,1)}), bf16[512,2048]{1,0:T(8,128)(2,1)}) %all-gather.41.cloned.1.call-update) | async-done | bytes 2097168 | tf_op jit(solution)/shard_map/all_gather | solution.py:304
  2373.0 64.3 %all-gather.43.cloned.1.call-done = bf16[512,3072]{0,1:T(8,128)(2,1)} async-done(((bf16[128,3072]{0,1:T(8,128)(2,1)}), bf16[512,3072]{0,1:T(8,128)(2,1)}) %all-gather.43.cloned.1.call-update) | async-done | bytes 3145744 | tf_op jit(solution)/shard_map/all_gather | solution.py:305
  2444.5 39.3 %all-gather.45.cloned.1.call-done = bf16[512,2048]{0,1:T(8,128)(2,1)} async-done(((bf16[128,2048]{0,1:T(8,128)(2,1)}), bf16[512,2048]{0,1:T(8,128)(2,1)}) %all-gather.45.cloned.1.call-update) | async-done | bytes 2097168 | tf_op jit(solution)/shard_map/all_gather | solution.py:302
  2483.8 46.2 %all-gather.47.cloned.1.call-done = bf16[512,2048]{1,0:T(8,128)(2,1)} async-done(((bf16[128,2048]{1,0:T(8,128)(2,1)}), bf16[512,2048]{1,0:T(8,128)(2,1)}) %all-gather.47.cloned.1.call-update) | async-done | bytes 2097168 | tf_op jit(solution)/shard_map/all_gather | solution.py:303
  2536.6 39.5 %all-gather.57.cloned.1.call-done = bf16[1,512,2048]{2,1,0:T(8,128)(2,1)} async-done(((bf16[1,128,2048]{2,1,0:T(8,128)(2,1)}), bf16[1,512,2048]{2,1,0:T(8,128)(2,1)}) %all-gather.57.cloned.1.call-update) | async-done | bytes 2097168 | tf_op jit(solution)/shard_map/all_gather | solution.py:213
  2576.1 149.8 %all-gather.53.cloned.1.call-done = bf16[512,8192]{1,0:T(8,128)(2,1)} async-done(((bf16[128,8192]{1,0:T(8,128)(2,1)}), bf16[512,8192]{1,0:T(8,128)(2,1)}) %all-gather.53.cloned.1.call-update) | async-done | bytes 8388624 | tf_op jit(solution)/shard_map/all_gather | solution.py:212
  2736.0 35.5 %all-gather.49.cloned.1.call-done = bf16[512,2048]{1,0:T(8,128)(2,1)} async-done(((bf16[128,2048]{1,0:T(8,128)(2,1)}), bf16[512,2048]{1,0:T(8,128)(2,1)}) %all-gather.49.cloned.1.call-update) | async-done | bytes 2097168 | tf_op jit(solution)/shard_map/all_gather | solution.py:214
  2771.5 287.7 %all-gather.51.cloned.1.call-done = bf16[512,16384]{1,0:T(8,128)(2,1)} async-done(((bf16[128,16384]{1,0:T(8,128)(2,1)}), bf16[512,16384]{1,0:T(8,128)(2,1)}) %all-gather.51.cloned.1.call-update) | async-done | bytes 16777232 | tf_op jit(solution)/shard_map/all_gather | solution.py:215
  3059.2 16.0 convolution_convert_fusion
  3095.3 19.5 fusion.65
  3117.5 15.7 all-reduce.2
  3133.4 12.4 all-reduce.3
  3162.5 337.5 %all-reduce.7.cloned.1.call-done = (bf16[512,512]{1,0:T(8,128)(2,1)}, bf16[512,512]{1,0:T(8,128)(2,1)}, bf16[512,2048]{1,0:T(8,128)(2,1)}, bf16[512,8192]{1,0:T(...) async-done(((bf16[512,512]{1,0:T(8,128)(2,1)}, bf16[512,512]{1,0:T(8,128)(2,1)}, bf16[512,2048]{1,0:T(8,128)(2,1)}, bf16[512,8192]{1,0:T(8,128)(2,1)}, ...) | async-done | bytes 28311568 | tf_op jit(solution)/shard_map/psum | solution.py:323
  (251 shorter events, 279.0 us)
Async XLA Ops:
  7.2 100.3 %copy-start.5 = (bf16[1,128,2048]{2,1,0:T(8,128)(2,1)S(1)}, bf16[1,128,2048]{2,1,0:T(8,128)(2,1)}, u32[]{:S(2)}) copy-start(bf16[1,128,2048]{2,1,0:T(8,128)(2,1)} %param.18) | copy-start | bytes 1572868
  7.2 51.1 %all-gather.23.cloned.1.call-start = ((), (), s32[]{:S(2)}) async-start(), calls=%async_computation.2 | async-start | bytes 2621440 | tf_op jit(solution)/shard_map/all_gather | solution.py:113
  7.9 96.6 %all-gather.27.cloned.1.call-start = ((), (), s32[]{:S(2)}) async-start(), calls=%async_computation.4 | async-start | bytes 2621440 | tf_op jit(solution)/shard_map/all_gather | solution.py:112
  8.7 120.6 %all-gather.25.cloned.1.call-start = ((), (), s32[]{:S(2)}) async-start(), calls=%async_computation.3 | async-start | bytes 1179648 | tf_op jit(solution)/shard_map/all_gather | solution.py:130
  23.0 295.7 %copy-start.23 = (f32[4,1,512]{2,1,0:T(1,128)}, f32[4,1,512]{2,1,0:T(1,128)S(1)}, u32[]{:S(2)}) copy-start(f32[4,1,512]{2,1,0:T(1,128)S(1)} %convert_element_type.205) | copy-start | bytes 24580
  24.2 294.4 %copy-start.28 = (f32[128]{0:T(128)}, f32[128]{0:T(128)S(1)}, u32[]{:S(2)}) copy-start(f32[128]{0:T(128)S(1)} %add_rsqrt_fusion.1) | copy-start | bytes 1540
  25.5 79.1 %copy-start.13 = (bf16[128,2048]{1,0:T(8,128)(2,1)}, bf16[128,2048]{1,0:T(8,128)(2,1)S(1)}, u32[]{:S(2)}) copy-start(bf16[128,2048]{1,0:T(8,128)(2,1)S(1)} %fusion.74) | copy-start | bytes 1572868
  61.0 94.1 %all-gather.29.cloned.1.call-start = ((), (), s32[]{:S(2)}) async-start(), calls=%async_computation.5 | async-start | bytes 1179648 | tf_op jit(solution)/shard_map/all_gather | solution.py:129
  62.3 262.5 %copy-start.18 = (f32[128,64]{0,1:T(8,128)}, f32[128,64]{0,1:T(8,128)S(1)}, u32[]{:S(2)}) copy-start(f32[128,64]{0,1:T(8,128)S(1)} %pad_maximum_fusion.5) | copy-start | bytes 98308
  62.3 262.5 %copy-start.20 = (f32[128,64]{0,1:T(8,128)}, f32[128,64]{0,1:T(8,128)S(1)}, u32[]{:S(2)}) copy-start(f32[128,64]{0,1:T(8,128)S(1)} %pad_maximum_fusion.4) | copy-start | bytes 98308
  109.0 197.2 %all-gather.31.cloned.1.call-start = ((), (), s32[]{:S(2)}) async-start(), calls=%async_computation.6 | async-start | bytes 10485760 | tf_op jit(solution)/shard_map/all_gather | solution.py:111
  109.6 345.9 %all-gather.33.cloned.1.call-start = ((), (), s32[]{:S(2)}) async-start(), calls=%async_computation.7 | async-start | bytes 10485760 | tf_op jit(solution)/shard_map/all_gather | solution.py:114
  110.2 906.6 %all-gather.35.cloned.1.call-start = ((), (), s32[]{:S(2)}) async-start(), calls=%async_computation.8 | async-start | bytes 41943040 | tf_op jit(solution)/shard_map/all_gather | solution.py:177
  110.9 1467.0 %all-gather.37.cloned.1.call-start = ((), (), s32[]{:S(2)}) async-start(), calls=%async_computation.9 | async-start | bytes 41943040 | tf_op jit(solution)/shard_map/all_gather | solution.py:178
  111.7 2027.5 %all-gather.39.cloned.1.call-start = ((), (), s32[]{:S(2)}) async-start(), calls=%async_computation.10 | async-start | bytes 41943040 | tf_op jit(solution)/shard_map/all_gather | solution.py:179
  112.4 2173.4 %reduce-scatter.7.cloned.1.call-start = ((), (), s32[]{:S(2)}) async-start(), calls=%async_computation.20 | async-start | bytes 1179648
  124.8 2071.5 %copy-start.25 = (f32[4,1,512]{2,1,0:T(1,128)}, f32[4,1,512]{2,1,0:T(1,128)S(1)}, u32[]{:S(2)}) copy-start(f32[4,1,512]{2,1,0:T(1,128)S(1)} %convert_element_type.206) | copy-start | bytes 24580
  460.5 1735.8 %copy-start.30 = (f32[128]{0:T(128)}, f32[128]{0:T(128)S(1)}, u32[]{:S(2)}) copy-start(f32[128]{0:T(128)S(1)} %add_rsqrt_fusion) | copy-start | bytes 1540
  461.7 1116.3 %copy-start.8 = (bf16[128,2048]{1,0:T(8,128)(2,1)}, bf16[128,2048]{1,0:T(8,128)(2,1)S(1)}, u32[]{:S(2)}) copy-start(bf16[128,2048]{1,0:T(8,128)(2,1)S(1)} %multiply_convert_fusion.3) | copy-start | bytes 1572868
  2251.5 74.2 %reduce-scatter.9.cloned.1.call-start = ((), (), s32[]{:S(2)}) async-start(), calls=%async_computation.21 | async-start | bytes 1179648
  2259.1 113.9 %all-gather.41.cloned.1.call-start = ((), (), s32[]{:S(2)}) async-start(), calls=%async_computation.11 | async-start | bytes 2621440 | tf_op jit(solution)/shard_map/all_gather | solution.py:304
  2259.6 177.7 %all-gather.43.cloned.1.call-start = ((), (), s32[]{:S(2)}) async-start(), calls=%async_computation.12 | async-start | bytes 3932160 | tf_op jit(solution)/shard_map/all_gather | solution.py:305
  2327.6 156.1 %all-gather.45.cloned.1.call-start = ((), (), s32[]{:S(2)}) async-start(), calls=%async_computation.13 | async-start | bytes 2621440 | tf_op jit(solution)/shard_map/all_gather | solution.py:302
  2328.2 201.8 %all-gather.47.cloned.1.call-start = ((), (), s32[]{:S(2)}) async-start(), calls=%async_computation.14 | async-start | bytes 2621440 | tf_op jit(solution)/shard_map/all_gather | solution.py:303
  2328.8 247.3 %all-gather.57.cloned.1.call-start = ((), (), s32[]{:S(2)}) async-start(), calls=%async_computation.19 | async-start | bytes 2621440 | tf_op jit(solution)/shard_map/all_gather | solution.py:213
  2329.4 396.5 %all-gather.53.cloned.1.call-start = ((), (), s32[]{:S(2)}) async-start(), calls=%async_computation.17 | async-start | bytes 10485760 | tf_op jit(solution)/shard_map/all_gather | solution.py:212
  2329.9 441.5 %all-gather.49.cloned.1.call-start = ((), (), s32[]{:S(2)}) async-start(), calls=%async_computation.15 | async-start | bytes 2621440 | tf_op jit(solution)/shard_map/all_gather | solution.py:214
  2330.5 728.6 %all-gather.51.cloned.1.call-start = ((), (), s32[]{:S(2)}) async-start(), calls=%async_computation.16 | async-start | bytes 20971520 | tf_op jit(solution)/shard_map/all_gather | solution.py:215
  2335.2 814.7 %all-gather.55.cloned.1.call-start = ((), (), s32[]{:S(2)}) async-start(), calls=%async_computation.18 | async-start | bytes 18874368 | tf_op jit(solution)/shard_map/all_gather | solution.py:319
  2444.4 1055.5 %all-reduce.7.cloned.1.call-start = ((), (), s32[]{:S(2)}) async-start(), calls=%async_computation.22 | async-start | bytes 56623104 | tf_op jit(solution)/shard_map/psum | solution.py:323
  3114.7 32.3 copy-start.7
  3114.7 32.3 copy-start.12
  (30 other events, 354.8 us)
Sparse Core Ops, SparseCore 0:
  9.6 48.6 all-gather.22
  59.8 44.6 all-gather.26
  107.0 22.1 all-gather.24
  131.5 23.5 all-gather.28
  156.5 149.6 all-gather.30
  307.6 147.8 all-gather.32
  457.1 559.6 all-gather.34
  1018.3 559.5 all-gather.36
  1579.5 559.5 all-gather.38
  2251.6 34.1 reduce-scatter.6
  2289.6 35.9 reduce-scatter.8
  2327.0 45.9 all-gather.40
  2375.1 62.1 all-gather.42
  2439.3 44.4 all-gather.44
  2485.7 44.1 all-gather.46
  2531.4 44.6 all-gather.56
  2577.5 148.3 all-gather.52
  2727.3 44.1 all-gather.48
  2773.6 285.4 all-gather.50
  3060.9 88.2 all-gather.54
  3155.2 344.7 all-reduce.6
